TPU v7x, 32 devices: a whole 2x2x4 slice. The times are simulated.
32 devices in a mesh: ctx: 8 (over z, y), head: 4 (over x, core).
Axes of the slice: x: 2, y: 2, z: 4, core: 2. Of those that a mesh axis runs over, the one named last changes fastest.
Arguments:
- queries: bfloat16 [2048, 6144], P(('ctx', 'head')), may hold values from -42 to 42
- key_head_columns: bfloat16 [2048, 512], P(('ctx', 'head')), may hold values from -4 to 4
- value_head_columns: bfloat16 [2048, 512], P(('ctx', 'head')), may hold values from -6 to 6
- output_gradient: bfloat16 [2048, 6144], P(('ctx', 'head')), may hold values from -6 to 6
- file_starts: int32 [5], replicated, may hold values from 0 to 1984, as said below
- file_imports: int32 [5, 4], replicated, may hold values from -1 to 4, as said below
- header_lens: int32 [5], replicated, may hold values from 16 to 64
Outputs:
- grad_queries: float32 [2048, 6144], P(('ctx', 'head'))
- key_gradient: float32 [2048, 512], P(('ctx', 'head'))
- value_gradient: float32 [2048, 512], P(('ctx', 'head'))
Inputs may be any that keep to these rules, and one draw needn't show every extreme that they name: `file_starts`: Increasing; the first is 0 and the last is 1984; each is a multiple of 64; no two lie in the same aligned block of 256 tokens; each file has 64 tokens or more. `file_imports`: each row lists distinct files other than its own, then -1 in the unused places; file 0 imports nothing.
All inputs are finite; a program needn't handle non-finite values.
Results may differ from a plain program's by a relative error of at most 0.004.
Values may be sent and summed in bfloat16 or wider, within the bound.
No kernel may reach another device: no remote copies, remote signals or barrier semaphores. Data moves between devices by JAX's collectives and lax.ppermute only.
A program may use at most 64 MiB of HBM per device.

v0:
```python
import math
import jax
import jax.numpy as jnp
from jax import lax
from jax.sharding import PartitionSpec as P

WIN = 1024
HDR = 64


def passed_along(value, axis, steps):
    count = lax.axis_size(axis)
    first, last = (max(0, -steps), min(count, count - steps))
    return lax.ppermute(value, axis, [(source, source + steps) for source in range(first, last)])


def local_files(file_starts, file_imports, header_lens, offset_base, span_rows):
    places = offset_base + jnp.arange(span_rows, dtype=jnp.int32)
    before = file_starts[None, :] <= places[:, None]
    file_of = jnp.sum(before.astype(jnp.int32), axis=1) - 1
    file_begin = jnp.max(jnp.where(before, file_starts[None, :], 0), axis=1)
    lower_file = file_of[0]
    upper_file = file_of[span_rows - 1]
    per_file = file_imports.shape[1]
    lower_list = lax.dynamic_slice_in_dim(file_imports, lower_file, 1, 0)[0]
    upper_list = lax.dynamic_slice_in_dim(file_imports, upper_file, 1, 0)[0]
    targets = jnp.concatenate([lower_list, upper_list])
    source_file = jnp.concatenate(
        [jnp.full((per_file,), lower_file, jnp.int32), jnp.full((per_file,), upper_file, jnp.int32)]
    )
    usable = (targets >= 0) & (
        (jnp.arange(2 * per_file, dtype=jnp.int32) < per_file) | (upper_file != lower_file)
    )
    matches = jnp.arange(file_starts.shape[0], dtype=jnp.int32)[None, :] == targets[:, None]
    target_start = jnp.sum(jnp.where(matches, file_starts[None, :], 0), axis=1)
    target_len = jnp.sum(jnp.where(matches, header_lens[None, :], 0), axis=1)
    return (places, file_of, file_begin, source_file, usable, target_start, target_len)


def visibility(places, file_of, file_begin, key_places, source_file, usable, target_len):
    window_ok = (
        (key_places[None, :] <= places[:, None])
        & (key_places[None, :] > places[:, None] - WIN)
        & (key_places[None, :] >= file_begin[:, None])
    )
    offsets = jnp.arange(usable.shape[0] * HDR, dtype=jnp.int32) % HDR
    header_ok = jnp.repeat(usable, HDR) & (offsets < jnp.repeat(target_len, HDR))
    header_vis = header_ok[None, :] & (file_of[:, None] == jnp.repeat(source_file, HDR)[None, :])
    return jnp.concatenate([window_ok, header_vis], axis=1)


def per_device(
    queries,
    key_head_columns,
    value_head_columns,
    output_gradient,
    file_starts,
    file_imports,
    header_lens,
):
    query_rows, key_rows, value_rows, grad_rows = (
        lax.all_to_all(queries, "head", split_axis=1, concat_axis=0, tiled=True),
        lax.all_to_all(key_head_columns, "head", split_axis=1, concat_axis=0, tiled=True),
        lax.all_to_all(value_head_columns, "head", split_axis=1, concat_axis=0, tiled=True),
        lax.all_to_all(output_gradient, "head", split_axis=1, concat_axis=0, tiled=True),
    )
    tokens_here = key_rows.shape[0]
    head_size = key_rows.shape[1]
    queries_per_group = query_rows.shape[1] // head_size
    shard_index = lax.axis_index("ctx")
    offset_base = shard_index * tokens_here
    scaling = 1.0 / math.sqrt(head_size)
    reach = WIN // tokens_here
    places, file_of, file_begin, source_file, usable, target_start, target_len = local_files(
        file_starts, file_imports, header_lens, offset_base, tokens_here
    )
    block_count = source_file.shape[0]
    stacked = jnp.concatenate([key_rows, value_rows], axis=1)
    earlier = []
    for distance in range(1, reach + 1):
        earlier.append(passed_along(stacked, "ctx", distance))
    inside = (file_starts >= offset_base) & (file_starts < offset_base + tokens_here)
    own_offset = jnp.sum(jnp.where(inside, file_starts - offset_base, 0))
    own_header = lax.dynamic_slice_in_dim(stacked, own_offset, HDR, 0)
    all_headers = lax.all_gather(own_header, "ctx", axis=0, tiled=True)
    header_rows = jnp.concatenate(
        [
            lax.dynamic_slice_in_dim(all_headers, target_start[index] // tokens_here * HDR, HDR, 0)
            for index in range(block_count)
        ],
        axis=0,
    )
    key_table = jnp.concatenate(earlier[::-1] + [stacked, header_rows], axis=0)
    key_matrix = key_table[:, :head_size]
    value_matrix = key_table[:, head_size:]
    window_len = (reach + 1) * tokens_here
    key_places = offset_base - reach * tokens_here + jnp.arange(window_len, dtype=jnp.int32)
    visible = visibility(places, file_of, file_begin, key_places, source_file, usable, target_len)
    heads_block = max(
        (
            divisor
            for divisor in range(1, queries_per_group + 1)
            if queries_per_group % divisor == 0 and divisor * tokens_here <= max(512, tokens_here)
        )
    )
    block_total = queries_per_group // heads_block
    query_blocks = (
        query_rows.reshape(tokens_here, queries_per_group, head_size)
        .transpose(1, 0, 2)
        .reshape(block_total, heads_block, tokens_here, head_size)
    )
    grad_blocks = (
        grad_rows.reshape(tokens_here, queries_per_group, head_size)
        .transpose(1, 0, 2)
        .reshape(block_total, heads_block, tokens_here, head_size)
    )

    def attend(carry, inputs):
        key_gradient_sum, value_gradient_sum = carry
        query_block, grad_block = inputs
        scores = (
            jnp.einsum("htd,kd->htk", query_block, key_matrix, preferred_element_type=jnp.float32)
            * scaling
        )
        scores = jnp.where(visible[None], scores, -jnp.inf)
        ceiling = jnp.max(scores, axis=-1, keepdims=True)
        log_total = ceiling + jnp.log(jnp.sum(jnp.exp(scores - ceiling), axis=-1, keepdims=True))
        weights = jnp.exp(scores - log_total)
        grad_weights = jnp.einsum(
            "htd,kd->htk", grad_block, value_matrix, preferred_element_type=jnp.float32
        )
        centre = jnp.sum(weights * grad_weights, axis=-1, keepdims=True)
        grad_scores = (weights * (grad_weights - centre)).astype(jnp.bfloat16)
        weights_low = weights.astype(jnp.bfloat16)
        grad_query = (
            jnp.einsum("htk,kd->htd", grad_scores, key_matrix, preferred_element_type=jnp.float32)
            * scaling
        )
        key_gradient_sum = (
            key_gradient_sum
            + jnp.einsum(
                "htk,htd->kd", grad_scores, query_block, preferred_element_type=jnp.float32
            )
            * scaling
        )
        value_gradient_sum = value_gradient_sum + jnp.einsum(
            "htk,htd->kd", weights_low, grad_block, preferred_element_type=jnp.float32
        )
        return ((key_gradient_sum, value_gradient_sum), grad_query)

    empty_gradient = jnp.zeros((key_table.shape[0], head_size), jnp.float32)
    (key_gradient_sum, value_gradient_sum), grad_query = lax.scan(
        attend, (empty_gradient, empty_gradient), (query_blocks, grad_blocks)
    )
    grad_query = (
        grad_query.reshape(queries_per_group, tokens_here, head_size)
        .transpose(1, 0, 2)
        .reshape(tokens_here, queries_per_group * head_size)
    )
    combined = jnp.concatenate([key_gradient_sum, value_gradient_sum], axis=1)

    def window_part(index):
        return combined[index * tokens_here : (index + 1) * tokens_here]

    collected = window_part(reach)
    for distance in range(1, reach + 1):
        collected = collected + passed_along(window_part(reach - distance), "ctx", -distance)
    header_part = combined[window_len:]
    blocks_out = header_part.reshape(block_count, HDR, 2 * head_size)
    holders = jnp.where(usable, target_start // tokens_here, -1)
    block_piece = lax.all_gather(blocks_out, "ctx", axis=0, tiled=True)
    holder_piece = lax.all_gather(holders, "ctx", axis=0, tiled=True)
    selected = (holder_piece == shard_index).astype(jnp.float32)
    arriving = jnp.einsum("m,mrc->rc", selected, block_piece)
    current = lax.dynamic_slice_in_dim(collected, own_offset, HDR, 0)
    collected = lax.dynamic_update_slice_in_dim(collected, current + arriving, own_offset, 0)
    grad_queries, key_gradient, value_gradient = (
        lax.all_to_all(grad_query, "head", split_axis=0, concat_axis=1, tiled=True),
        lax.all_to_all(collected[:, :head_size], "head", split_axis=0, concat_axis=1, tiled=True),
        lax.all_to_all(collected[:, head_size:], "head", split_axis=0, concat_axis=1, tiled=True),
    )
    return (grad_queries, key_gradient, value_gradient)


def solution(mesh):
    in_specs = (
        P(("ctx", "head"), None),
        P(("ctx", "head"), None),
        P(("ctx", "head"), None),
        P(("ctx", "head"), None),
        P(),
        P(),
        P(),
    )
    out_specs = (P(("ctx", "head"), None), P(("ctx", "head"), None), P(("ctx", "head"), None))
    return jax.shard_map(
        per_device, mesh=mesh, in_specs=in_specs, out_specs=out_specs, check_vma=False
    )
```

profile of v0, /device:TPU:0, one launch (start us, length us, event | category | flops | bytes accessed | tf_op | source)
XLA Modules:
  0.0 296.5 jit_solution(10358402667834652991)
XLA Ops:
  8.7 4.2 %all-to-all-start.1 = ((bf16[64,4,128]{2,0,1:T(8,128)(2,1)}), bf16[64,4,128]{2,0,1:T(8,128)(2,1)S(1)}, u32[]{:S(2)}, u32[]{:S(2)}) async-start(bf16[64,4,128]{2,0,1:T(8,128)(2,1)} %copy_bitcast_fusion.6), calls=%async_computation.1 | async-start | bytes 131072 | tf_op jit(solution)/shard_map/all_to_all | solution.py:63
  18.2 1.5 copy_bitcast_fusion.5
  28.4 3.3 %all-to-all-start.2 = ((bf16[64,4,128]{2,0,1:T(8,128)(2,1)}), bf16[64,4,128]{2,0,1:T(8,128)(2,1)S(1)}, u32[]{:S(2)}, u32[]{:S(2)}) async-start(bf16[64,4,128]{2,0,1:T(8,128)(2,1)} %copy_bitcast_fusion.5), calls=%async_computation.2 | async-start | bytes 131072 | tf_op jit(solution)/shard_map/all_to_all | solution.py:64
  31.7 1.4 fusion.41
  57.7 3.5 %all-to-all-start.3 = ((bf16[64,4,1536]{2,0,1:T(8,128)(2,1)}), bf16[64,4,1536]{2,0,1:T(8,128)(2,1)S(1)}, u32[]{:S(2)}, u32[]{:S(2)}) async-start(bf16[64,4,1536]{2,0,1:T(8,128)(2,1)} %bitcast.142), calls=%async_computation.3 | async-start | bytes 1572864 | tf_op jit(solution)/shard_map/all_to_all | solution.py:65
  61.2 5.0 %collective-permute-start = (bf16[256,256]{1,0:T(8,128)(2,1)S(1)}, bf16[256,256]{1,0:T(8,128)(2,1)S(1)}, u32[]{:S(2)}, u32[]{:S(2)}) collective-permute-start(bf16[256,256]{1,0:T(8,128)(2,1)S(1)} %pad_maximum_fusion), channel_id=1, source_target_pairs={{0,16},{4,20},{8,24},{12,28},{1,17},{5,21},{9,25},{13,29},{2,18},{... | collective-permute-start | bytes 393224 | tf_op jit(solution)/shard_map/ppermute | solution.py:14
  66.2 4.4 %collective-permute-start.1 = (bf16[256,256]{1,0:T(8,128)(2,1)S(1)}, bf16[256,256]{1,0:T(8,128)(2,1)S(1)}, u32[]{:S(2)}, u32[]{:S(2)}) collective-permute-start(bf16[256,256]{1,0:T(8,128)(2,1)S(1)} %pad_maximum_fusion), channel_id=1, source_target_pairs={{0,12},{4,16},{8,20},{12,24},{16,28},{1,13},{5,17},{9,21},{13,25},... | collective-permute-start | bytes 393224 | tf_op jit(solution)/shard_map/ppermute | solution.py:14
  72.0 3.1 %collective-permute-start.3 = (bf16[256,256]{1,0:T(8,128)(2,1)S(1)}, bf16[256,256]{1,0:T(8,128)(2,1)S(1)}, u32[]{:S(2)}, u32[]{:S(2)}) collective-permute-start(bf16[256,256]{1,0:T(8,128)(2,1)S(1)} %pad_maximum_fusion), channel_id=1, source_target_pairs={{0,4},{4,8},{8,12},{12,16},{16,20},{20,24},{24,28},{1,5},{5,9},{9,... | collective-permute-start | bytes 393224 | tf_op jit(solution)/shard_map/ppermute | solution.py:14
  75.1 31.9 %all_gather.9 = bf16[512,256]{1,0:T(8,128)(2,1)S(1)} all-gather(bf16[64,256]{1,0:T(8,128)(2,1)S(1)} %fusion.29), channel_id=1, replica_groups=mesh['ctx'=8,'head'=4] {'ctx'}, dimensions={0}, use_global_device_ids=true | all-gather | bytes 294912 | tf_op jit(solution)/shard_map/all_gather | solution.py:85
  114.7 4.2 %all-to-all-start = ((bf16[64,4,1536]{2,0,1:T(8,128)(2,1)}), bf16[64,4,1536]{2,0,1:T(8,128)(2,1)}, u32[]{:S(2)}, u32[]{:S(2)}) async-start(bf16[64,4,1536]{2,0,1:T(8,128)(2,1)} %bitcast.141), calls=%async_computation | async-start | bytes 1572864 | tf_op jit(solution)/shard_map/all_to_all | solution.py:62
  120.8 1.5 reshape.109
  122.3 1.4 copy.68
  123.7 6.8 %all-to-all-done = bf16[64,4,1536]{2,0,1:T(8,128)(2,1)} async-done(((bf16[64,4,1536]{2,0,1:T(8,128)(2,1)}), bf16[64,4,1536]{2,0,1:T(8,128)(2,1)}, u32[]{:S(2)}, u32[]{:S(2)}) %all-to-all-start) | async-done | bytes 786464 | tf_op jit(solution)/shard_map/all_to_all | solution.py:62
  130.6 2.4 reshape.107
  133.0 2.3 copy.64
  135.3 68.0 %while.15 = (s32[]{:T(128)}, f32[1792,128]{1,0:T(8,128)S(1)}, f32[1792,128]{1,0:T(8,128)}, f32[6,2,256,128]{3,2,1,0:T(8,128)}, pred[256,1792]{1,0:T(8,128)(4,1)S...) while((s32[]{:T(128)}, f32[1792,128]{1,0:T(8,128)S(1)}, ...), condition=%wide.region_9.10_spmd.clone, body=%wide.region_5.9_spmd.clone.sunk | while | flops 1188461568 | bytes 80503144 | solution.py:152
  135.3 2.0 fusion.71
  139.9 1.4 fusion.74
  141.2 2.1 fusion.72
  143.4 2.9 fusion.73
  146.3 2.0 fusion.71
  150.9 1.4 fusion.74
  152.3 2.1 fusion.72
  154.4 3.3 %fusion.73 = f32[1792,128]{1,0:T(8,128)} fusion(f32[2,256,1792]{2,1,0:T(8,128)S(1)} %copy-done.2, f32[2,256]{1,0:T(2,128)S(1)} %log_add_fusion.2, f32[1792,128]{1,0:T(8,128)} %get-tuple-element.220, pred[]{:T(512)S(6)} %compare.23, bf16[6,2,256,128]{3,2,1,0:T(8,128)(2,1)} %copy-done.8, s32[]{:T(128)} %get-tuple-element.218), kind=kOutput, calls=%fused_computation.10.clone.1 | convolution fusion | flops 237174784 | bytes 5638657 | tf_op jit(solution)/shard_map/while/body/eval_jaxpr/htk,htd->kd/dot_general | solution.py:146
  157.7 2.0 fusion.71
  162.3 1.4 fusion.74
  163.7 2.1 fusion.72
  165.8 3.3 %fusion.73 = f32[1792,128]{1,0:T(8,128)} fusion(f32[2,256,1792]{2,1,0:T(8,128)S(1)} %copy-done.2, f32[2,256]{1,0:T(2,128)S(1)} %log_add_fusion.2, f32[1792,128]{1,0:T(8,128)} %get-tuple-element.220, pred[]{:T(512)S(6)} %compare.23, bf16[6,2,256,128]{3,2,1,0:T(8,128)(2,1)} %copy-done.8, s32[]{:T(128)} %get-tuple-element.218), kind=kOutput, calls=%fused_computation.10.clone.1 | convolution fusion | flops 237174784 | bytes 5638657 | tf_op jit(solution)/shard_map/while/body/eval_jaxpr/htk,htd->kd/dot_general | solution.py:146
  169.1 2.0 fusion.71
  173.7 1.4 fusion.74
  175.1 2.1 fusion.72
  177.2 3.3 %fusion.73 = f32[1792,128]{1,0:T(8,128)} fusion(f32[2,256,1792]{2,1,0:T(8,128)S(1)} %copy-done.2, f32[2,256]{1,0:T(2,128)S(1)} %log_add_fusion.2, f32[1792,128]{1,0:T(8,128)} %get-tuple-element.220, pred[]{:T(512)S(6)} %compare.23, bf16[6,2,256,128]{3,2,1,0:T(8,128)(2,1)} %copy-done.8, s32[]{:T(128)} %get-tuple-element.218), kind=kOutput, calls=%fused_computation.10.clone.1 | convolution fusion | flops 237174784 | bytes 5638657 | tf_op jit(solution)/shard_map/while/body/eval_jaxpr/htk,htd->kd/dot_general | solution.py:146
  180.5 2.0 fusion.71
  186.5 2.1 fusion.72
  188.6 3.3 %fusion.73 = f32[1792,128]{1,0:T(8,128)} fusion(f32[2,256,1792]{2,1,0:T(8,128)S(1)} %copy-done.2, f32[2,256]{1,0:T(2,128)S(1)} %log_add_fusion.2, f32[1792,128]{1,0:T(8,128)} %get-tuple-element.220, pred[]{:T(512)S(6)} %compare.23, bf16[6,2,256,128]{3,2,1,0:T(8,128)(2,1)} %copy-done.8, s32[]{:T(128)} %get-tuple-element.218), kind=kOutput, calls=%fused_computation.10.clone.1 | convolution fusion | flops 237174784 | bytes 5638657 | tf_op jit(solution)/shard_map/while/body/eval_jaxpr/htk,htd->kd/dot_general | solution.py:146
  191.9 2.0 fusion.71
  197.9 2.1 fusion.72
  200.0 3.3 %fusion.73 = f32[1792,128]{1,0:T(8,128)} fusion(f32[2,256,1792]{2,1,0:T(8,128)S(1)} %copy-done.2, f32[2,256]{1,0:T(2,128)S(1)} %log_add_fusion.2, f32[1792,128]{1,0:T(8,128)} %get-tuple-element.220, pred[]{:T(512)S(6)} %compare.23, bf16[6,2,256,128]{3,2,1,0:T(8,128)(2,1)} %copy-done.8, s32[]{:T(128)} %get-tuple-element.218), kind=kOutput, calls=%fused_computation.10.clone.1 | convolution fusion | flops 237174784 | bytes 5638657 | tf_op jit(solution)/shard_map/while/body/eval_jaxpr/htk,htd->kd/dot_general | solution.py:146
  210.3 1.5 collective-permute-start.7
  211.8 2.4 copy.94
  214.2 1.4 all_to_all.108
  215.5 3.6 %all-to-all-start.4 = ((f32[4,64,1536]{2,1,0:T(8,128)}), f32[4,64,1536]{2,1,0:T(8,128)S(1)}, u32[]{:S(2)}, u32[]{:S(2)}) async-start(f32[4,64,1536]{2,1,0:T(8,128)} %all_to_all.108), calls=%async_computation.4 | async-start | bytes 3145728 | tf_op jit(solution)/shard_map/all_to_all | solution.py:178
  219.1 48.7 %all-reduce.1 = s32[64]{0:T(128)S(1)} all-reduce(s32[64]{0:T(128)S(1)} %get-tuple-element.118), channel_id=1, replica_groups=mesh['ctx'=8,'head'=4] {'ctx'}, use_global_device_ids=true, to_apply=%add.1 | all-reduce | flops 64 | bytes 512
  269.1 2.8 fusion.24
  273.2 3.3 %all-to-all-start.6 = ((f32[4,64,128]{2,1,0:T(8,128)}), f32[4,64,128]{2,1,0:T(8,128)S(1)}, u32[]{:S(2)}, u32[]{:S(2)}) async-start(f32[4,64,128]{2,1,0:T(8,128)} %bitcast.29), calls=%async_computation.6 | async-start | bytes 262144 | tf_op jit(solution)/shard_map/all_to_all | solution.py:180
  277.8 3.3 %all-to-all-done.6 = f32[4,64,128]{2,1,0:T(8,128)S(1)} async-done(((f32[4,64,128]{2,1,0:T(8,128)}), f32[4,64,128]{2,1,0:T(8,128)S(1)}, u32[]{:S(2)}, u32[]{:S(2)}) %all-to-all-start.6) | async-done | bytes 131104 | tf_op jit(solution)/shard_map/all_to_all | solution.py:180
  281.1 3.3 %all-to-all-start.5 = ((f32[4,64,128]{2,1,0:T(8,128)}), f32[4,64,128]{2,1,0:T(8,128)S(1)}, u32[]{:S(2)}, u32[]{:S(2)}) async-start(f32[4,64,128]{2,1,0:T(8,128)} %bitcast.27), calls=%async_computation.5 | async-start | bytes 262144 | tf_op jit(solution)/shard_map/all_to_all | solution.py:179
  285.1 3.9 %all-to-all-done.5 = f32[4,64,128]{2,1,0:T(8,128)S(1)} async-done(((f32[4,64,128]{2,1,0:T(8,128)}), f32[4,64,128]{2,1,0:T(8,128)S(1)}, u32[]{:S(2)}, u32[]{:S(2)}) %all-to-all-start.5) | async-done | bytes 131104 | tf_op jit(solution)/shard_map/all_to_all | solution.py:179
  (208 shorter events, 52.6 us)
Async XLA Ops:
  7.2 47.8 %copy-start.11 = (bf16[64,6144]{1,0:T(8,128)(2,1)S(1)}, bf16[64,6144]{1,0:T(8,128)(2,1)}, u32[]{:S(2)}) copy-start(bf16[64,6144]{1,0:T(8,128)(2,1)} %param.12) | copy-start | bytes 2359300
  8.0 47.9 %copy-start.12 = (bf16[64,6144]{1,0:T(8,128)(2,1)S(1)}, bf16[64,6144]{1,0:T(8,128)(2,1)}, u32[]{:S(2)}) copy-start(bf16[64,6144]{1,0:T(8,128)(2,1)} %param.9) | copy-start | bytes 2359300
  8.7 19.7 %all-to-all-start.1 = ((bf16[64,4,128]{2,0,1:T(8,128)(2,1)}), bf16[64,4,128]{2,0,1:T(8,128)(2,1)S(1)}, u32[]{:S(2)}, u32[]{:S(2)}) async-start(bf16[64,4,128]{2,0,1:T(8,128)(2,1)} %copy_bitcast_fusion.6), calls=%async_computation.1 | async-start | bytes 131072 | tf_op jit(solution)/shard_map/all_to_all | solution.py:63
  28.4 29.3 %all-to-all-start.2 = ((bf16[64,4,128]{2,0,1:T(8,128)(2,1)}), bf16[64,4,128]{2,0,1:T(8,128)(2,1)S(1)}, u32[]{:S(2)}, u32[]{:S(2)}) async-start(bf16[64,4,128]{2,0,1:T(8,128)(2,1)} %copy_bitcast_fusion.5), calls=%async_computation.2 | async-start | bytes 131072 | tf_op jit(solution)/shard_map/all_to_all | solution.py:64
  57.7 57.0 %all-to-all-start.3 = ((bf16[64,4,1536]{2,0,1:T(8,128)(2,1)}), bf16[64,4,1536]{2,0,1:T(8,128)(2,1)S(1)}, u32[]{:S(2)}, u32[]{:S(2)}) async-start(bf16[64,4,1536]{2,0,1:T(8,128)(2,1)} %bitcast.142), calls=%async_computation.3 | async-start | bytes 1572864 | tf_op jit(solution)/shard_map/all_to_all | solution.py:65
  61.2 45.8 %collective-permute-start = (bf16[256,256]{1,0:T(8,128)(2,1)S(1)}, bf16[256,256]{1,0:T(8,128)(2,1)S(1)}, u32[]{:S(2)}, u32[]{:S(2)}) collective-permute-start(bf16[256,256]{1,0:T(8,128)(2,1)S(1)} %pad_maximum_fusion), channel_id=1, source_target_pairs={{0,16},{4,20},{8,24},{12,28},{1,17},{5,21},{9,25},{13,29},{2,18},{... | collective-permute-start | bytes 393224 | tf_op jit(solution)/shard_map/ppermute | solution.py:14
  66.2 41.5 %collective-permute-start.1 = (bf16[256,256]{1,0:T(8,128)(2,1)S(1)}, bf16[256,256]{1,0:T(8,128)(2,1)S(1)}, u32[]{:S(2)}, u32[]{:S(2)}) collective-permute-start(bf16[256,256]{1,0:T(8,128)(2,1)S(1)} %pad_maximum_fusion), channel_id=1, source_target_pairs={{0,12},{4,16},{8,20},{12,24},{16,28},{1,13},{5,17},{9,21},{13,25},... | collective-permute-start | bytes 393224 | tf_op jit(solution)/shard_map/ppermute | solution.py:14
  70.7 37.7 %collective-permute-start.2 = (bf16[256,256]{1,0:T(8,128)(2,1)S(1)}, bf16[256,256]{1,0:T(8,128)(2,1)S(1)}, u32[]{:S(2)}, u32[]{:S(2)}) collective-permute-start(bf16[256,256]{1,0:T(8,128)(2,1)S(1)} %pad_maximum_fusion), channel_id=1, source_target_pairs={{0,8},{4,12},{8,16},{12,20},{16,24},{20,28},{1,9},{5,13},{9,17},{1... | collective-permute-start | bytes 393224 | tf_op jit(solution)/shard_map/ppermute | solution.py:14
  72.0 37.0 %collective-permute-start.3 = (bf16[256,256]{1,0:T(8,128)(2,1)S(1)}, bf16[256,256]{1,0:T(8,128)(2,1)S(1)}, u32[]{:S(2)}, u32[]{:S(2)}) collective-permute-start(bf16[256,256]{1,0:T(8,128)(2,1)S(1)} %pad_maximum_fusion), channel_id=1, source_target_pairs={{0,4},{4,8},{8,12},{12,16},{16,20},{20,24},{24,28},{1,5},{5,9},{9,... | collective-permute-start | bytes 393224 | tf_op jit(solution)/shard_map/ppermute | solution.py:14
  114.7 15.9 %all-to-all-start = ((bf16[64,4,1536]{2,0,1:T(8,128)(2,1)}), bf16[64,4,1536]{2,0,1:T(8,128)(2,1)}, u32[]{:S(2)}, u32[]{:S(2)}) async-start(bf16[64,4,1536]{2,0,1:T(8,128)(2,1)} %bitcast.141), calls=%async_computation | async-start | bytes 1572864 | tf_op jit(solution)/shard_map/all_to_all | solution.py:62
  118.9 150.2 %all-gather.2.cloned.1.call-start = ((), (), s32[]{:S(2)}) async-start(), calls=%async_computation.7 | async-start | bytes 2359296 | tf_op jit(solution)/shard_map/all_gather | solution.py:171
  135.3 3.6 %copy-start.8 = (bf16[6,2,256,128]{3,2,1,0:T(8,128)(2,1)}, bf16[6,2,256,128]{3,2,1,0:T(8,128)(2,1)S(1)}, u32[]{:S(2)}) copy-start(bf16[6,2,256,128]{3,2,1,0:T(8,128)(2,1)S(1)} %get-tuple-element.236) | copy-start | bytes 2359300 | tf_op jit(solution)/shard_map/while
  143.3 3.0 %copy-start.5 = (pred[256,1792]{1,0:T(8,128)(4,1)S(1)}, pred[256,1792]{1,0:T(8,128)(4,1)}, u32[]{:S(2)}) copy-start(pred[256,1792]{1,0:T(8,128)(4,1)} %copy-done.4) | copy-start | bytes 1376260 | tf_op jit(solution)/shard_map/while
  143.3 3.0 %copy-start.7 = (bf16[1792,128]{1,0:T(8,128)(2,1)S(1)}, bf16[1792,128]{1,0:T(8,128)(2,1)}, u32[]{:S(2)}) copy-start(bf16[1792,128]{1,0:T(8,128)(2,1)} %copy-done.6) | copy-start | bytes 1376260 | tf_op jit(solution)/shard_map/while
  143.3 3.0 copy-start.9
  146.3 2.7 copy-start.6
  146.3 3.6 %copy-start.8 = (bf16[6,2,256,128]{3,2,1,0:T(8,128)(2,1)}, bf16[6,2,256,128]{3,2,1,0:T(8,128)(2,1)S(1)}, u32[]{:S(2)}) copy-start(bf16[6,2,256,128]{3,2,1,0:T(8,128)(2,1)S(1)} %get-tuple-element.236) | copy-start | bytes 2359300 | tf_op jit(solution)/shard_map/while
  154.4 3.3 %copy-start.5 = (pred[256,1792]{1,0:T(8,128)(4,1)S(1)}, pred[256,1792]{1,0:T(8,128)(4,1)}, u32[]{:S(2)}) copy-start(pred[256,1792]{1,0:T(8,128)(4,1)} %copy-done.4) | copy-start | bytes 1376260 | tf_op jit(solution)/shard_map/while
  154.4 3.3 %copy-start.7 = (bf16[1792,128]{1,0:T(8,128)(2,1)S(1)}, bf16[1792,128]{1,0:T(8,128)(2,1)}, u32[]{:S(2)}) copy-start(bf16[1792,128]{1,0:T(8,128)(2,1)} %copy-done.6) | copy-start | bytes 1376260 | tf_op jit(solution)/shard_map/while
  154.4 3.3 %copy-start.9 = (bf16[6,2,256,128]{3,2,1,0:T(8,128)(2,1)S(1)}, bf16[6,2,256,128]{3,2,1,0:T(8,128)(2,1)}, u32[]{:S(2)}) copy-start(bf16[6,2,256,128]{3,2,1,0:T(8,128)(2,1)} %copy-done.8) | copy-start | bytes 2359300 | tf_op jit(solution)/shard_map/while
  157.7 2.7 copy-start.6
  157.7 3.6 %copy-start.8 = (bf16[6,2,256,128]{3,2,1,0:T(8,128)(2,1)}, bf16[6,2,256,128]{3,2,1,0:T(8,128)(2,1)S(1)}, u32[]{:S(2)}) copy-start(bf16[6,2,256,128]{3,2,1,0:T(8,128)(2,1)S(1)} %get-tuple-element.236) | copy-start | bytes 2359300 | tf_op jit(solution)/shard_map/while
  165.8 3.3 %copy-start.5 = (pred[256,1792]{1,0:T(8,128)(4,1)S(1)}, pred[256,1792]{1,0:T(8,128)(4,1)}, u32[]{:S(2)}) copy-start(pred[256,1792]{1,0:T(8,128)(4,1)} %copy-done.4) | copy-start | bytes 1376260 | tf_op jit(solution)/shard_map/while
  165.8 3.3 %copy-start.7 = (bf16[1792,128]{1,0:T(8,128)(2,1)S(1)}, bf16[1792,128]{1,0:T(8,128)(2,1)}, u32[]{:S(2)}) copy-start(bf16[1792,128]{1,0:T(8,128)(2,1)} %copy-done.6) | copy-start | bytes 1376260 | tf_op jit(solution)/shard_map/while
  165.8 3.3 %copy-start.9 = (bf16[6,2,256,128]{3,2,1,0:T(8,128)(2,1)S(1)}, bf16[6,2,256,128]{3,2,1,0:T(8,128)(2,1)}, u32[]{:S(2)}) copy-start(bf16[6,2,256,128]{3,2,1,0:T(8,128)(2,1)} %copy-done.8) | copy-start | bytes 2359300 | tf_op jit(solution)/shard_map/while
  169.1 2.7 copy-start.6
  169.1 3.6 %copy-start.8 = (bf16[6,2,256,128]{3,2,1,0:T(8,128)(2,1)}, bf16[6,2,256,128]{3,2,1,0:T(8,128)(2,1)S(1)}, u32[]{:S(2)}) copy-start(bf16[6,2,256,128]{3,2,1,0:T(8,128)(2,1)S(1)} %get-tuple-element.236) | copy-start | bytes 2359300 | tf_op jit(solution)/shard_map/while
  177.2 3.3 %copy-start.5 = (pred[256,1792]{1,0:T(8,128)(4,1)S(1)}, pred[256,1792]{1,0:T(8,128)(4,1)}, u32[]{:S(2)}) copy-start(pred[256,1792]{1,0:T(8,128)(4,1)} %copy-done.4) | copy-start | bytes 1376260 | tf_op jit(solution)/shard_map/while
  177.2 3.3 %copy-start.7 = (bf16[1792,128]{1,0:T(8,128)(2,1)S(1)}, bf16[1792,128]{1,0:T(8,128)(2,1)}, u32[]{:S(2)}) copy-start(bf16[1792,128]{1,0:T(8,128)(2,1)} %copy-done.6) | copy-start | bytes 1376260 | tf_op jit(solution)/shard_map/while
  177.2 3.3 %copy-start.9 = (bf16[6,2,256,128]{3,2,1,0:T(8,128)(2,1)S(1)}, bf16[6,2,256,128]{3,2,1,0:T(8,128)(2,1)}, u32[]{:S(2)}) copy-start(bf16[6,2,256,128]{3,2,1,0:T(8,128)(2,1)} %copy-done.8) | copy-start | bytes 2359300 | tf_op jit(solution)/shard_map/while
  180.5 2.7 copy-start.6
  180.5 3.6 %copy-start.8 = (bf16[6,2,256,128]{3,2,1,0:T(8,128)(2,1)}, bf16[6,2,256,128]{3,2,1,0:T(8,128)(2,1)S(1)}, u32[]{:S(2)}) copy-start(bf16[6,2,256,128]{3,2,1,0:T(8,128)(2,1)S(1)} %get-tuple-element.236) | copy-start | bytes 2359300 | tf_op jit(solution)/shard_map/while
  188.6 3.3 %copy-start.5 = (pred[256,1792]{1,0:T(8,128)(4,1)S(1)}, pred[256,1792]{1,0:T(8,128)(4,1)}, u32[]{:S(2)}) copy-start(pred[256,1792]{1,0:T(8,128)(4,1)} %copy-done.4) | copy-start | bytes 1376260 | tf_op jit(solution)/shard_map/while
  188.6 3.3 %copy-start.7 = (bf16[1792,128]{1,0:T(8,128)(2,1)S(1)}, bf16[1792,128]{1,0:T(8,128)(2,1)}, u32[]{:S(2)}) copy-start(bf16[1792,128]{1,0:T(8,128)(2,1)} %copy-done.6) | copy-start | bytes 1376260 | tf_op jit(solution)/shard_map/while
  188.6 3.3 %copy-start.9 = (bf16[6,2,256,128]{3,2,1,0:T(8,128)(2,1)S(1)}, bf16[6,2,256,128]{3,2,1,0:T(8,128)(2,1)}, u32[]{:S(2)}) copy-start(bf16[6,2,256,128]{3,2,1,0:T(8,128)(2,1)} %copy-done.8) | copy-start | bytes 2359300 | tf_op jit(solution)/shard_map/while
  191.9 2.7 copy-start.6
  191.9 3.6 %copy-start.8 = (bf16[6,2,256,128]{3,2,1,0:T(8,128)(2,1)}, bf16[6,2,256,128]{3,2,1,0:T(8,128)(2,1)S(1)}, u32[]{:S(2)}) copy-start(bf16[6,2,256,128]{3,2,1,0:T(8,128)(2,1)S(1)} %get-tuple-element.236) | copy-start | bytes 2359300 | tf_op jit(solution)/shard_map/while
  200.0 3.3 %copy-start.5 = (pred[256,1792]{1,0:T(8,128)(4,1)S(1)}, pred[256,1792]{1,0:T(8,128)(4,1)}, u32[]{:S(2)}) copy-start(pred[256,1792]{1,0:T(8,128)(4,1)} %copy-done.4) | copy-start | bytes 1376260 | tf_op jit(solution)/shard_map/while
  200.0 3.3 %copy-start.7 = (bf16[1792,128]{1,0:T(8,128)(2,1)S(1)}, bf16[1792,128]{1,0:T(8,128)(2,1)}, u32[]{:S(2)}) copy-start(bf16[1792,128]{1,0:T(8,128)(2,1)} %copy-done.6) | copy-start | bytes 1376260 | tf_op jit(solution)/shard_map/while
  200.0 3.3 %copy-start.9 = (bf16[6,2,256,128]{3,2,1,0:T(8,128)(2,1)S(1)}, bf16[6,2,256,128]{3,2,1,0:T(8,128)(2,1)}, u32[]{:S(2)}) copy-start(bf16[6,2,256,128]{3,2,1,0:T(8,128)(2,1)} %copy-done.8) | copy-start | bytes 2359300 | tf_op jit(solution)/shard_map/while
  204.5 7.3 %copy-start.10 = (f32[1792,256]{1,0:T(8,128)}, f32[1792,256]{1,0:T(8,128)S(1)}, u32[]{:S(2)}) copy-start(f32[1792,256]{1,0:T(8,128)S(1)} %constant_dynamic-update-slice_fusion.13) | copy-start | bytes 5505028
  206.4 61.4 %collective-permute-start.4 = (f32[256,256]{1,0:T(8,128)}, f32[256,256]{1,0:T(8,128)S(1)}, u32[]{:S(2)}, u32[]{:S(2)}) collective-permute-start(f32[256,256]{1,0:T(8,128)} %get-tuple-element.124), channel_id=1, source_target_pairs={{4,0},{8,4},{12,8},{16,12},{20,16},{24,20},{28,24},{5,1},{9,5},{13... | collective-permute-start | bytes 786440 | tf_op jit(solution)/shard_map/ppermute | solution.py:14
  207.7 60.1 %collective-permute-start.5 = (f32[256,256]{1,0:T(8,128)}, f32[256,256]{1,0:T(8,128)S(1)}, u32[]{:S(2)}, u32[]{:S(2)}) collective-permute-start(f32[256,256]{1,0:T(8,128)} %get-tuple-element.127), channel_id=1, source_target_pairs={{8,0},{12,4},{16,8},{20,12},{24,16},{28,20},{9,1},{13,5},{17,9},{2... | collective-permute-start | bytes 786440 | tf_op jit(solution)/shard_map/ppermute | solution.py:14
  209.0 58.8 %collective-permute-start.6 = (f32[256,256]{1,0:T(8,128)}, f32[256,256]{1,0:T(8,128)}, u32[]{:S(2)}, u32[]{:S(2)}) collective-permute-start(f32[256,256]{1,0:T(8,128)} %get-tuple-element.126), channel_id=1, source_target_pairs={{12,0},{16,4},{20,8},{24,12},{28,16},{13,1},{17,5},{21,9},{25,13},... | collective-permute-start | bytes 786440 | tf_op jit(solution)/shard_map/ppermute | solution.py:14
  210.3 57.5 %collective-permute-start.7 = (f32[256,256]{1,0:T(8,128)}, f32[256,256]{1,0:T(8,128)}, u32[]{:S(2)}, u32[]{:S(2)}) collective-permute-start(f32[256,256]{1,0:T(8,128)} %get-tuple-element.125), channel_id=1, source_target_pairs={{16,0},{20,4},{24,8},{28,12},{17,1},{21,5},{25,9},{29,13},{18,2},{... | collective-permute-start | bytes 786440 | tf_op jit(solution)/shard_map/ppermute | solution.py:14
  215.5 57.6 %all-to-all-start.4 = ((f32[4,64,1536]{2,1,0:T(8,128)}), f32[4,64,1536]{2,1,0:T(8,128)S(1)}, u32[]{:S(2)}, u32[]{:S(2)}) async-start(f32[4,64,1536]{2,1,0:T(8,128)} %all_to_all.108), calls=%async_computation.4 | async-start | bytes 3145728 | tf_op jit(solution)/shard_map/all_to_all | solution.py:178
  273.2 7.9 %all-to-all-start.6 = ((f32[4,64,128]{2,1,0:T(8,128)}), f32[4,64,128]{2,1,0:T(8,128)S(1)}, u32[]{:S(2)}, u32[]{:S(2)}) async-start(f32[4,64,128]{2,1,0:T(8,128)} %bitcast.29), calls=%async_computation.6 | async-start | bytes 262144 | tf_op jit(solution)/shard_map/all_to_all | solution.py:180
  281.1 7.9 %all-to-all-start.5 = ((f32[4,64,128]{2,1,0:T(8,128)}), f32[4,64,128]{2,1,0:T(8,128)S(1)}, u32[]{:S(2)}, u32[]{:S(2)}) async-start(f32[4,64,128]{2,1,0:T(8,128)} %bitcast.27), calls=%async_computation.5 | async-start | bytes 262144 | tf_op jit(solution)/shard_map/all_to_all | solution.py:179
  (21 other events, 40.0 us)
Sparse Core Ops, SparseCore 0:
  205.5 60.7 all-gather.1
where the time goes:
time: 299 us; the launch traced here: 296 us
  blocking collectives  80.6 us (27%)
  matrix products  60.3 us (20%)
  starting transfers between devices  44.7 us (15%)
  between operations  43 us (14%)
  local copies, waits for them, and re-layouts  38.6 us (13%)
  other arithmetic  14.6 us (5%)
  waiting for transfers between devices  14.1 us (5%)
    unnamed x1, blocking collectives  48.7 us
    all_gather x1, blocking collectives, per_device(): all_headers = lax.all_gather(own_header, 'ctx', axis=0, tiled=True)  31.9 us
    dot_general x6, matrix products, attend(): jnp.einsum('htk,htd->kd', weights_low, grad_block, preferred_element_type...  19.3 us
    ppermute x8, starting transfers between devices, passed_along(): lax.ppermute(value, axis, [(source, source + steps) for source in range(f...  19.2 us
    dot_general x6, matrix products, attend(): jnp.einsum('htk,htd->kd', grad_scores, query_block, preferred_element_typ...  12.4 us
    dot_general x6, matrix products, attend(): jnp.einsum('htd,kd->htk', query_block, key_matrix, preferred_element_type...  11.8 us
    unnamed x24, local copies, waits for them, and re-layouts  10.3 us
    dot_general x6, matrix products, attend(): jnp.einsum('htk,kd->htd', grad_scores, key_matrix, preferred_element_type...  8.1 us
  transfers between devices with their start and end apart: 16, of which 3 were waited for; matrix products, arithmetic and copies ran while one was open for 12% of the time, Pallas kernels for 0%

commit v1 on v0

--- a/solution.py
+++ b/solution.py
@@ -82,7 +82,13 @@
     inside = (file_starts >= offset_base) & (file_starts < offset_base + tokens_here)
     own_offset = jnp.sum(jnp.where(inside, file_starts - offset_base, 0))
     own_header = lax.dynamic_slice_in_dim(stacked, own_offset, HDR, 0)
-    all_headers = lax.all_gather(own_header, "ctx", axis=0, tiled=True)
+    size = lax.axis_size("ctx")
+    held, tiles = (own_header, [own_header])
+    for _ in range(size - 1):
+        held = lax.ppermute(held, "ctx", [(i, (i + 1) % size) for i in range(size)])
+        tiles.insert(0, held)
+    row_of_blocks = jnp.concatenate(tiles, axis=0)
+    all_headers = jnp.roll(row_of_blocks, (lax.axis_index("ctx") + 1) * own_header.shape[0], axis=0)
     header_rows = jnp.concatenate(
         [
             lax.dynamic_slice_in_dim(all_headers, target_start[index] // tokens_here * HDR, HDR, 0)

time: 299 us -> 300 us (level)
  blocking collectives: 80.6 us -> 38.5 us
  waiting for transfers between devices: 14.1 us -> 45.2 us
  starting transfers between devices: 44.7 us -> 53.5 us
  local copies, waits for them, and re-layouts: 38.6 us -> 41.8 us
    all_gather x1 -> x0, blocking collectives: 31.9 us -> none  [per_device(): all_headers = lax.all_gather(own_header, 'ctx', axis=0, tiled=True)]
    ppermute x0 -> x7, waiting for transfers between devices: none -> 26.2 us  [per_device(): held = lax.ppermute(held, 'ctx', [(i, (i + 1) % size) for i in range(size)])]
    unnamed x1, blocking collectives: 48.7 us -> 38.5 us
    all_gather x1, waiting for transfers between devices: 0.02 us -> 5.71 us  [per_device(): block_piece = lax.all_gather(blocks_out, 'ctx', axis=0, tiled=True)]
    ppermute x8, starting transfers between devices: 19.2 us -> 24.8 us  [passed_along(): lax.ppermute(value, axis, [(source, source + steps) for source in range(f...]
    ppermute x0 -> x7, starting transfers between devices: none -> 3.25 us  [per_device(): held = lax.ppermute(held, 'ctx', [(i, (i + 1) % size) for i in range(size)])]
    unnamed x24 -> x37, local copies, waits for them, and re-layouts: 10.3 us -> 10.5 us
  transfers between devices with their start and end apart: 16 -> 23, of which waited for: 3 -> 10; matrix products, arithmetic and copies ran while one was open for 12% -> 13% of each run, Pallas kernels for 0% -> 0%
where the time goes in v1:
time: 300 us; the launch traced here: 298 us
  matrix products  60.3 us (20%)
  starting transfers between devices  53.5 us (18%)
  waiting for transfers between devices  45.2 us (15%)
  between operations  43.2 us (14%)
  local copies, waits for them, and re-layouts  41.8 us (14%)
  blocking collectives  38.5 us (13%)
  other arithmetic  14.5 us (5%)
    unnamed x1, blocking collectives  38.5 us
    ppermute x7, waiting for transfers between devices, per_device(): held = lax.ppermute(held, 'ctx', [(i, (i + 1) % size) for i in range(size)])  26.2 us
    ppermute x8, starting transfers between devices, passed_along(): lax.ppermute(value, axis, [(source, source + steps) for source in range(f...  24.8 us
    dot_general x6, matrix products, attend(): jnp.einsum('htk,htd->kd', weights_low, grad_block, preferred_element_type...  19.2 us
    dot_general x6, matrix products, attend(): jnp.einsum('htk,htd->kd', grad_scores, query_block, preferred_element_typ...  12.5 us
    dot_general x6, matrix products, attend(): jnp.einsum('htd,kd->htk', query_block, key_matrix, preferred_element_type...  11.9 us
    unnamed x37, local copies, waits for them, and re-layouts  10.5 us
    dot_general x6, matrix products, attend(): jnp.einsum('htk,kd->htd', grad_scores, key_matrix, preferred_element_type...  8.1 us
  transfers between devices with their start and end apart: 23, of which 10 were waited for; matrix products, arithmetic and copies ran while one was open for 13% of the time, Pallas kernels for 0%

profile of v1, /device:TPU:0, one launch (start us, length us, event | category | flops | bytes accessed | tf_op | source)
XLA Modules:
  0.0 297.5 jit_solution(8920483604327314060)
XLA Ops:
  8.7 4.2 %all-to-all-start.1 = ((bf16[64,4,128]{2,0,1:T(8,128)(2,1)}), bf16[64,4,128]{2,0,1:T(8,128)(2,1)S(1)}, u32[]{:S(2)}, u32[]{:S(2)}) async-start(bf16[64,4,128]{2,0,1:T(8,128)(2,1)} %copy_bitcast_fusion.6), calls=%async_computation.1 | async-start | bytes 131072 | tf_op jit(solution)/shard_map/all_to_all | solution.py:63
  27.3 3.3 %all-to-all-start.2 = ((bf16[64,4,128]{2,0,1:T(8,128)(2,1)}), bf16[64,4,128]{2,0,1:T(8,128)(2,1)S(1)}, u32[]{:S(2)}, u32[]{:S(2)}) async-start(bf16[64,4,128]{2,0,1:T(8,128)(2,1)} %copy_bitcast_fusion.5), calls=%async_computation.2 | async-start | bytes 131072 | tf_op jit(solution)/shard_map/all_to_all | solution.py:64
  33.2 2.1 copy.95
  36.0 3.5 %all-to-all-start.3 = ((bf16[64,4,1536]{2,0,1:T(8,128)(2,1)}), bf16[64,4,1536]{2,0,1:T(8,128)(2,1)S(1)}, u32[]{:S(2)}, u32[]{:S(2)}) async-start(bf16[64,4,1536]{2,0,1:T(8,128)(2,1)} %bitcast.108), calls=%async_computation.3 | async-start | bytes 1572864 | tf_op jit(solution)/shard_map/all_to_all | solution.py:65
  39.5 2.1 collective-permute-start.4
  41.7 4.5 %collective-permute-start = (bf16[256,256]{1,0:T(8,128)(2,1)S(1)}, bf16[256,256]{1,0:T(8,128)(2,1)S(1)}, u32[]{:S(2)}, u32[]{:S(2)}) collective-permute-start(bf16[256,256]{1,0:T(8,128)(2,1)S(1)} %pad_maximum_fusion), channel_id=1, source_target_pairs={{0,16},{4,20},{8,24},{12,28},{1,17},{5,21},{9,25},{13,29},{2,18},{... | collective-permute-start | bytes 393224 | tf_op jit(solution)/shard_map/ppermute | solution.py:14
  47.8 3.1 %collective-permute-start.1 = (bf16[256,256]{1,0:T(8,128)(2,1)S(1)}, bf16[256,256]{1,0:T(8,128)(2,1)S(1)}, u32[]{:S(2)}, u32[]{:S(2)}) collective-permute-start(bf16[256,256]{1,0:T(8,128)(2,1)S(1)} %pad_maximum_fusion), channel_id=1, source_target_pairs={{0,12},{4,16},{8,20},{12,24},{16,28},{1,13},{5,17},{9,21},{13,25},... | collective-permute-start | bytes 393224 | tf_op jit(solution)/shard_map/ppermute | solution.py:14
  50.9 2.4 collective-permute-done.5
  75.0 2.1 copy.96
  77.1 6.5 %collective-permute-start.2 = (bf16[256,256]{1,0:T(8,128)(2,1)S(1)}, bf16[256,256]{1,0:T(8,128)(2,1)S(1)}, u32[]{:S(2)}, u32[]{:S(2)}) collective-permute-start(bf16[256,256]{1,0:T(8,128)(2,1)S(1)} %pad_maximum_fusion), channel_id=1, source_target_pairs={{0,8},{4,12},{8,16},{12,20},{16,24},{20,28},{1,9},{5,13},{9,17},{1... | collective-permute-start | bytes 393224 | tf_op jit(solution)/shard_map/ppermute | solution.py:14
  83.7 5.3 %collective-permute-start.3 = (bf16[256,256]{1,0:T(8,128)(2,1)S(1)}, bf16[256,256]{1,0:T(8,128)(2,1)S(1)}, u32[]{:S(2)}, u32[]{:S(2)}) collective-permute-start(bf16[256,256]{1,0:T(8,128)(2,1)S(1)} %pad_maximum_fusion), channel_id=1, source_target_pairs={{0,4},{4,8},{8,12},{12,16},{16,20},{20,24},{24,28},{1,5},{5,9},{9,... | collective-permute-start | bytes 393224 | tf_op jit(solution)/shard_map/ppermute | solution.py:14
  90.4 5.3 %collective-permute-done.7 = bf16[64,256]{1,0:T(8,128)(2,1)S(1)} collective-permute-done((bf16[64,256]{1,0:T(8,128)(2,1)S(1)}, bf16[64,256]{1,0:T(8,128)(2,1)S(1)}, u32[]{:S(2)}, u32[]{:S(2)}) %collective-permute-start.7) | collective-permute-done | bytes 32800 | tf_op jit(solution)/shard_map/ppermute | solution.py:88
  96.3 5.9 %collective-permute-done.8 = bf16[64,256]{1,0:T(8,128)(2,1)S(1)} collective-permute-done((bf16[64,256]{1,0:T(8,128)(2,1)S(1)}, bf16[64,256]{1,0:T(8,128)(2,1)S(1)}, u32[]{:S(2)}, u32[]{:S(2)}) %collective-permute-start.8) | collective-permute-done | bytes 32800 | tf_op jit(solution)/shard_map/ppermute | solution.py:88
  102.9 6.1 %collective-permute-done.9 = bf16[64,256]{1,0:T(8,128)(2,1)S(1)} collective-permute-done((bf16[64,256]{1,0:T(8,128)(2,1)S(1)}, bf16[64,256]{1,0:T(8,128)(2,1)S(1)}, u32[]{:S(2)}, u32[]{:S(2)}) %collective-permute-start.9) | collective-permute-done | bytes 32800 | tf_op jit(solution)/shard_map/ppermute | solution.py:88
  109.7 5.9 %collective-permute-done.10 = bf16[64,256]{1,0:T(8,128)(2,1)S(1)} collective-permute-done((bf16[64,256]{1,0:T(8,128)(2,1)S(1)}, bf16[64,256]{1,0:T(8,128)(2,1)S(1)}, u32[]{:S(2)}, u32[]{:S(2)}) %collective-permute-start.10) | collective-permute-done | bytes 32800 | tf_op jit(solution)/shard_map/ppermute | solution.py:88
  120.4 4.2 %all-to-all-start = ((bf16[64,4,1536]{2,0,1:T(8,128)(2,1)}), bf16[64,4,1536]{2,0,1:T(8,128)(2,1)}, u32[]{:S(2)}, u32[]{:S(2)}) async-start(bf16[64,4,1536]{2,0,1:T(8,128)(2,1)} %bitcast.141), calls=%async_computation | async-start | bytes 1572864 | tf_op jit(solution)/shard_map/all_to_all | solution.py:62
  127.2 1.5 reshape.109
  130.2 6.1 %all-to-all-done = bf16[64,4,1536]{2,0,1:T(8,128)(2,1)} async-done(((bf16[64,4,1536]{2,0,1:T(8,128)(2,1)}), bf16[64,4,1536]{2,0,1:T(8,128)(2,1)}, u32[]{:S(2)}, u32[]{:S(2)}) %all-to-all-start) | async-done | bytes 786464 | tf_op jit(solution)/shard_map/all_to_all | solution.py:62
  136.2 2.4 reshape.107
  138.6 2.3 copy.64
  141.0 68.0 %while.15 = (s32[]{:T(128)}, f32[1792,128]{1,0:T(8,128)S(1)}, f32[1792,128]{1,0:T(8,128)}, f32[6,2,256,128]{3,2,1,0:T(8,128)}, pred[256,1792]{1,0:T(8,128)(4,1)S...) while((s32[]{:T(128)}, f32[1792,128]{1,0:T(8,128)S(1)}, ...), condition=%wide.region_9.10_spmd.clone, body=%wide.region_5.9_spmd.clone.sunk | while | flops 1188461568 | bytes 80503144 | solution.py:158
  141.0 2.0 fusion.71
  146.9 2.1 fusion.72
  149.0 2.9 fusion.73
  152.0 2.0 fusion.71
  157.9 2.1 fusion.72
  160.1 3.3 %fusion.73 = f32[1792,128]{1,0:T(8,128)} fusion(f32[2,256,1792]{2,1,0:T(8,128)S(1)} %copy-done.2, f32[2,256]{1,0:T(2,128)S(1)} %log_add_fusion.2, f32[1792,128]{1,0:T(8,128)} %get-tuple-element.220, pred[]{:T(512)S(6)} %compare.24, bf16[6,2,256,128]{3,2,1,0:T(8,128)(2,1)} %copy-done.8, s32[]{:T(128)} %get-tuple-element.218), kind=kOutput, calls=%fused_computation.10.clone.1 | convolution fusion | flops 237174784 | bytes 5638657 | tf_op jit(solution)/shard_map/while/body/eval_jaxpr/htk,htd->kd/dot_general | solution.py:152
  163.4 2.0 fusion.71
  169.3 2.1 fusion.72
  171.5 3.3 %fusion.73 = f32[1792,128]{1,0:T(8,128)} fusion(f32[2,256,1792]{2,1,0:T(8,128)S(1)} %copy-done.2, f32[2,256]{1,0:T(2,128)S(1)} %log_add_fusion.2, f32[1792,128]{1,0:T(8,128)} %get-tuple-element.220, pred[]{:T(512)S(6)} %compare.24, bf16[6,2,256,128]{3,2,1,0:T(8,128)(2,1)} %copy-done.8, s32[]{:T(128)} %get-tuple-element.218), kind=kOutput, calls=%fused_computation.10.clone.1 | convolution fusion | flops 237174784 | bytes 5638657 | tf_op jit(solution)/shard_map/while/body/eval_jaxpr/htk,htd->kd/dot_general | solution.py:152
  174.8 2.0 fusion.71
  180.7 2.1 fusion.72
  182.9 3.3 %fusion.73 = f32[1792,128]{1,0:T(8,128)} fusion(f32[2,256,1792]{2,1,0:T(8,128)S(1)} %copy-done.2, f32[2,256]{1,0:T(2,128)S(1)} %log_add_fusion.2, f32[1792,128]{1,0:T(8,128)} %get-tuple-element.220, pred[]{:T(512)S(6)} %compare.24, bf16[6,2,256,128]{3,2,1,0:T(8,128)(2,1)} %copy-done.8, s32[]{:T(128)} %get-tuple-element.218), kind=kOutput, calls=%fused_computation.10.clone.1 | convolution fusion | flops 237174784 | bytes 5638657 | tf_op jit(solution)/shard_map/while/body/eval_jaxpr/htk,htd->kd/dot_general | solution.py:152
  186.2 2.0 fusion.71
  192.1 2.1 fusion.72
  194.3 3.3 %fusion.73 = f32[1792,128]{1,0:T(8,128)} fusion(f32[2,256,1792]{2,1,0:T(8,128)S(1)} %copy-done.2, f32[2,256]{1,0:T(2,128)S(1)} %log_add_fusion.2, f32[1792,128]{1,0:T(8,128)} %get-tuple-element.220, pred[]{:T(512)S(6)} %compare.24, bf16[6,2,256,128]{3,2,1,0:T(8,128)(2,1)} %copy-done.8, s32[]{:T(128)} %get-tuple-element.218), kind=kOutput, calls=%fused_computation.10.clone.1 | convolution fusion | flops 237174784 | bytes 5638657 | tf_op jit(solution)/shard_map/while/body/eval_jaxpr/htk,htd->kd/dot_general | solution.py:152
  197.6 2.0 fusion.71
  203.5 2.1 fusion.72
  205.6 3.3 %fusion.73 = f32[1792,128]{1,0:T(8,128)} fusion(f32[2,256,1792]{2,1,0:T(8,128)S(1)} %copy-done.2, f32[2,256]{1,0:T(2,128)S(1)} %log_add_fusion.2, f32[1792,128]{1,0:T(8,128)} %get-tuple-element.220, pred[]{:T(512)S(6)} %compare.24, bf16[6,2,256,128]{3,2,1,0:T(8,128)(2,1)} %copy-done.8, s32[]{:T(128)} %get-tuple-element.218), kind=kOutput, calls=%fused_computation.10.clone.1 | convolution fusion | flops 237174784 | bytes 5638657 | tf_op jit(solution)/shard_map/while/body/eval_jaxpr/htk,htd->kd/dot_general | solution.py:152
  217.4 2.4 copy.94
  221.1 3.6 %all-to-all-start.4 = ((f32[4,64,1536]{2,1,0:T(8,128)}), f32[4,64,1536]{2,1,0:T(8,128)S(1)}, u32[]{:S(2)}, u32[]{:S(2)}) async-start(f32[4,64,1536]{2,1,0:T(8,128)} %all_to_all.108), calls=%async_computation.4 | async-start | bytes 3145728 | tf_op jit(solution)/shard_map/all_to_all | solution.py:184
  224.7 38.5 %all-reduce.1 = s32[64]{0:T(128)S(1)} all-reduce(s32[64]{0:T(128)S(1)} %get-tuple-element.118), channel_id=1, replica_groups=mesh['ctx'=8,'head'=4] {'ctx'}, use_global_device_ids=true, to_apply=%add.1 | all-reduce | flops 64 | bytes 512
  264.4 5.7 %all-gather.2.cloned.1.call-done = bf16[64,64,256]{2,1,0:T(8,128)(2,1)} async-done(((bf16[8,64,256]{2,1,0:T(8,128)(2,1)}), bf16[64,64,256]{2,1,0:T(8,128)(2,1)}) %all-gather.2.cloned.1.call-update) | async-done | bytes 2097168 | tf_op jit(solution)/shard_map/all_gather | solution.py:177
  270.1 2.8 fusion.24
  274.2 3.3 %all-to-all-start.6 = ((f32[4,64,128]{2,1,0:T(8,128)}), f32[4,64,128]{2,1,0:T(8,128)S(1)}, u32[]{:S(2)}, u32[]{:S(2)}) async-start(f32[4,64,128]{2,1,0:T(8,128)} %bitcast.29), calls=%async_computation.6 | async-start | bytes 262144 | tf_op jit(solution)/shard_map/all_to_all | solution.py:186
  278.8 3.3 %all-to-all-done.6 = f32[4,64,128]{2,1,0:T(8,128)S(1)} async-done(((f32[4,64,128]{2,1,0:T(8,128)}), f32[4,64,128]{2,1,0:T(8,128)S(1)}, u32[]{:S(2)}, u32[]{:S(2)}) %all-to-all-start.6) | async-done | bytes 131104 | tf_op jit(solution)/shard_map/all_to_all | solution.py:186
  282.1 3.3 %all-to-all-start.5 = ((f32[4,64,128]{2,1,0:T(8,128)}), f32[4,64,128]{2,1,0:T(8,128)S(1)}, u32[]{:S(2)}, u32[]{:S(2)}) async-start(f32[4,64,128]{2,1,0:T(8,128)} %bitcast.27), calls=%async_computation.5 | async-start | bytes 262144 | tf_op jit(solution)/shard_map/all_to_all | solution.py:185
  286.1 3.9 %all-to-all-done.5 = f32[4,64,128]{2,1,0:T(8,128)S(1)} async-done(((f32[4,64,128]{2,1,0:T(8,128)}), f32[4,64,128]{2,1,0:T(8,128)S(1)}, u32[]{:S(2)}, u32[]{:S(2)}) %all-to-all-start.5) | async-done | bytes 131104 | tf_op jit(solution)/shard_map/all_to_all | solution.py:185
  (235 shorter events, 64.3 us)
Async XLA Ops:
  8.7 18.6 %all-to-all-start.1 = ((bf16[64,4,128]{2,0,1:T(8,128)(2,1)}), bf16[64,4,128]{2,0,1:T(8,128)(2,1)S(1)}, u32[]{:S(2)}, u32[]{:S(2)}) async-start(bf16[64,4,128]{2,0,1:T(8,128)(2,1)} %copy_bitcast_fusion.6), calls=%async_computation.1 | async-start | bytes 131072 | tf_op jit(solution)/shard_map/all_to_all | solution.py:63
  27.3 8.7 %all-to-all-start.2 = ((bf16[64,4,128]{2,0,1:T(8,128)(2,1)}), bf16[64,4,128]{2,0,1:T(8,128)(2,1)S(1)}, u32[]{:S(2)}, u32[]{:S(2)}) async-start(bf16[64,4,128]{2,0,1:T(8,128)(2,1)} %copy_bitcast_fusion.5), calls=%async_computation.2 | async-start | bytes 131072 | tf_op jit(solution)/shard_map/all_to_all | solution.py:64
  36.0 84.4 %all-to-all-start.3 = ((bf16[64,4,1536]{2,0,1:T(8,128)(2,1)}), bf16[64,4,1536]{2,0,1:T(8,128)(2,1)S(1)}, u32[]{:S(2)}, u32[]{:S(2)}) async-start(bf16[64,4,1536]{2,0,1:T(8,128)(2,1)} %bitcast.108), calls=%async_computation.3 | async-start | bytes 1572864 | tf_op jit(solution)/shard_map/all_to_all | solution.py:65
  39.5 7.2 %collective-permute-start.4 = (bf16[64,256]{1,0:T(8,128)(2,1)S(1)}, bf16[64,256]{1,0:T(8,128)(2,1)S(1)}, u32[]{:S(2)}, u32[]{:S(2)}) collective-permute-start(bf16[64,256]{1,0:T(8,128)(2,1)S(1)} %fusion.29), channel_id=1, source_target_pairs={{0,4},{4,8},{8,12},{12,16},{16,20},{20,24},{24,28},{28,0},{1,5},{5... | collective-permute-start | bytes 98312 | tf_op jit(solution)/shard_map/ppermute | solution.py:88
  41.7 47.4 %collective-permute-start = (bf16[256,256]{1,0:T(8,128)(2,1)S(1)}, bf16[256,256]{1,0:T(8,128)(2,1)S(1)}, u32[]{:S(2)}, u32[]{:S(2)}) collective-permute-start(bf16[256,256]{1,0:T(8,128)(2,1)S(1)} %pad_maximum_fusion), channel_id=1, source_target_pairs={{0,16},{4,20},{8,24},{12,28},{1,17},{5,21},{9,25},{13,29},{2,18},{... | collective-permute-start | bytes 393224 | tf_op jit(solution)/shard_map/ppermute | solution.py:14
  46.7 6.6 %collective-permute-start.5 = (bf16[64,256]{1,0:T(8,128)(2,1)S(1)}, bf16[64,256]{1,0:T(8,128)(2,1)S(1)}, u32[]{:S(2)}, u32[]{:S(2)}) collective-permute-start(bf16[64,256]{1,0:T(8,128)(2,1)S(1)} %collective-permute-done.4), channel_id=1, source_target_pairs={{0,4},{4,8},{8,12},{12,16},{16,20},{20,24},{24,28},{28,0},{1,5},{5... | collective-permute-start | bytes 98312 | tf_op jit(solution)/shard_map/ppermute | solution.py:88
  47.8 41.9 %collective-permute-start.1 = (bf16[256,256]{1,0:T(8,128)(2,1)S(1)}, bf16[256,256]{1,0:T(8,128)(2,1)S(1)}, u32[]{:S(2)}, u32[]{:S(2)}) collective-permute-start(bf16[256,256]{1,0:T(8,128)(2,1)S(1)} %pad_maximum_fusion), channel_id=1, source_target_pairs={{0,12},{4,16},{8,20},{12,24},{16,28},{1,13},{5,17},{9,21},{13,25},... | collective-permute-start | bytes 393224 | tf_op jit(solution)/shard_map/ppermute | solution.py:14
  53.3 35.7 %collective-permute-start.6 = (bf16[64,256]{1,0:T(8,128)(2,1)S(1)}, bf16[64,256]{1,0:T(8,128)(2,1)S(1)}, u32[]{:S(2)}, u32[]{:S(2)}) collective-permute-start(bf16[64,256]{1,0:T(8,128)(2,1)S(1)} %collective-permute-done.5), channel_id=1, source_target_pairs={{0,4},{4,8},{8,12},{12,16},{16,20},{20,24},{24,28},{28,0},{1,5},{5... | collective-permute-start | bytes 98312 | tf_op jit(solution)/shard_map/ppermute | solution.py:88
  77.1 18.5 %collective-permute-start.2 = (bf16[256,256]{1,0:T(8,128)(2,1)S(1)}, bf16[256,256]{1,0:T(8,128)(2,1)S(1)}, u32[]{:S(2)}, u32[]{:S(2)}) collective-permute-start(bf16[256,256]{1,0:T(8,128)(2,1)S(1)} %pad_maximum_fusion), channel_id=1, source_target_pairs={{0,8},{4,12},{8,16},{12,20},{16,24},{20,28},{1,9},{5,13},{9,17},{1... | collective-permute-start | bytes 393224 | tf_op jit(solution)/shard_map/ppermute | solution.py:14
  83.7 18.6 %collective-permute-start.3 = (bf16[256,256]{1,0:T(8,128)(2,1)S(1)}, bf16[256,256]{1,0:T(8,128)(2,1)S(1)}, u32[]{:S(2)}, u32[]{:S(2)}) collective-permute-start(bf16[256,256]{1,0:T(8,128)(2,1)S(1)} %pad_maximum_fusion), channel_id=1, source_target_pairs={{0,4},{4,8},{8,12},{12,16},{16,20},{20,24},{24,28},{1,5},{5,9},{9,... | collective-permute-start | bytes 393224 | tf_op jit(solution)/shard_map/ppermute | solution.py:14
  89.0 6.7 %collective-permute-start.7 = (bf16[64,256]{1,0:T(8,128)(2,1)S(1)}, bf16[64,256]{1,0:T(8,128)(2,1)S(1)}, u32[]{:S(2)}, u32[]{:S(2)}) collective-permute-start(bf16[64,256]{1,0:T(8,128)(2,1)S(1)} %collective-permute-done.6), channel_id=1, source_target_pairs={{0,4},{4,8},{8,12},{12,16},{16,20},{20,24},{24,28},{28,0},{1,5},{5... | collective-permute-start | bytes 98312 | tf_op jit(solution)/shard_map/ppermute | solution.py:88
  95.6 6.6 %collective-permute-start.8 = (bf16[64,256]{1,0:T(8,128)(2,1)S(1)}, bf16[64,256]{1,0:T(8,128)(2,1)S(1)}, u32[]{:S(2)}, u32[]{:S(2)}) collective-permute-start(bf16[64,256]{1,0:T(8,128)(2,1)S(1)} %collective-permute-done.7), channel_id=1, source_target_pairs={{0,4},{4,8},{8,12},{12,16},{16,20},{20,24},{24,28},{28,0},{1,5},{5... | collective-permute-start | bytes 98312 | tf_op jit(solution)/shard_map/ppermute | solution.py:88
  102.3 6.8 %collective-permute-start.9 = (bf16[64,256]{1,0:T(8,128)(2,1)S(1)}, bf16[64,256]{1,0:T(8,128)(2,1)S(1)}, u32[]{:S(2)}, u32[]{:S(2)}) collective-permute-start(bf16[64,256]{1,0:T(8,128)(2,1)S(1)} %collective-permute-done.8), channel_id=1, source_target_pairs={{0,4},{4,8},{8,12},{12,16},{16,20},{20,24},{24,28},{28,0},{1,5},{5... | collective-permute-start | bytes 98312 | tf_op jit(solution)/shard_map/ppermute | solution.py:88
  109.1 6.6 %collective-permute-start.10 = (bf16[64,256]{1,0:T(8,128)(2,1)S(1)}, bf16[64,256]{1,0:T(8,128)(2,1)S(1)}, u32[]{:S(2)}, u32[]{:S(2)}) collective-permute-start(bf16[64,256]{1,0:T(8,128)(2,1)S(1)} %collective-permute-done.9), channel_id=1, source_target_pairs={{0,4},{4,8},{8,12},{12,16},{16,20},{20,24},{24,28},{28,0},{1,5},{5... | collective-permute-start | bytes 98312 | tf_op jit(solution)/shard_map/ppermute | solution.py:88
  115.9 3.9 %copy-start.11 = (bf16[1024,256]{1,0:T(8,128)(2,1)}, bf16[1024,256]{1,0:T(8,128)(2,1)S(1)}, u32[]{:S(2)}) copy-start(bf16[1024,256]{1,0:T(8,128)(2,1)S(1)} %constant_dynamic-update-slice_fusion) | copy-start | bytes 1572868
  120.4 15.9 %all-to-all-start = ((bf16[64,4,1536]{2,0,1:T(8,128)(2,1)}), bf16[64,4,1536]{2,0,1:T(8,128)(2,1)}, u32[]{:S(2)}, u32[]{:S(2)}) async-start(bf16[64,4,1536]{2,0,1:T(8,128)(2,1)} %bitcast.141), calls=%async_computation | async-start | bytes 1572864 | tf_op jit(solution)/shard_map/all_to_all | solution.py:62
  124.6 145.6 %all-gather.2.cloned.1.call-start = ((), (), s32[]{:S(2)}) async-start(), calls=%async_computation.7 | async-start | bytes 2359296 | tf_op jit(solution)/shard_map/all_gather | solution.py:177
  141.0 3.6 %copy-start.8 = (bf16[6,2,256,128]{3,2,1,0:T(8,128)(2,1)}, bf16[6,2,256,128]{3,2,1,0:T(8,128)(2,1)S(1)}, u32[]{:S(2)}) copy-start(bf16[6,2,256,128]{3,2,1,0:T(8,128)(2,1)S(1)} %get-tuple-element.236) | copy-start | bytes 2359300 | tf_op jit(solution)/shard_map/while
  149.0 3.0 copy-start.5
  149.0 3.0 copy-start.7
  152.0 3.6 %copy-start.8 = (bf16[6,2,256,128]{3,2,1,0:T(8,128)(2,1)}, bf16[6,2,256,128]{3,2,1,0:T(8,128)(2,1)S(1)}, u32[]{:S(2)}) copy-start(bf16[6,2,256,128]{3,2,1,0:T(8,128)(2,1)S(1)} %get-tuple-element.236) | copy-start | bytes 2359300 | tf_op jit(solution)/shard_map/while
  160.0 3.3 %copy-start.5 = (pred[256,1792]{1,0:T(8,128)(4,1)S(1)}, pred[256,1792]{1,0:T(8,128)(4,1)}, u32[]{:S(2)}) copy-start(pred[256,1792]{1,0:T(8,128)(4,1)} %copy-done.4) | copy-start | bytes 1376260 | tf_op jit(solution)/shard_map/while
  160.1 3.3 %copy-start.7 = (bf16[1792,128]{1,0:T(8,128)(2,1)S(1)}, bf16[1792,128]{1,0:T(8,128)(2,1)}, u32[]{:S(2)}) copy-start(bf16[1792,128]{1,0:T(8,128)(2,1)} %copy-done.6) | copy-start | bytes 1376260 | tf_op jit(solution)/shard_map/while
  160.1 3.3 %copy-start.9 = (bf16[6,2,256,128]{3,2,1,0:T(8,128)(2,1)S(1)}, bf16[6,2,256,128]{3,2,1,0:T(8,128)(2,1)}, u32[]{:S(2)}) copy-start(bf16[6,2,256,128]{3,2,1,0:T(8,128)(2,1)} %copy-done.8) | copy-start | bytes 2359300 | tf_op jit(solution)/shard_map/while
  163.4 3.6 %copy-start.8 = (bf16[6,2,256,128]{3,2,1,0:T(8,128)(2,1)}, bf16[6,2,256,128]{3,2,1,0:T(8,128)(2,1)S(1)}, u32[]{:S(2)}) copy-start(bf16[6,2,256,128]{3,2,1,0:T(8,128)(2,1)S(1)} %get-tuple-element.236) | copy-start | bytes 2359300 | tf_op jit(solution)/shard_map/while
  171.4 3.3 %copy-start.5 = (pred[256,1792]{1,0:T(8,128)(4,1)S(1)}, pred[256,1792]{1,0:T(8,128)(4,1)}, u32[]{:S(2)}) copy-start(pred[256,1792]{1,0:T(8,128)(4,1)} %copy-done.4) | copy-start | bytes 1376260 | tf_op jit(solution)/shard_map/while
  171.4 3.3 %copy-start.7 = (bf16[1792,128]{1,0:T(8,128)(2,1)S(1)}, bf16[1792,128]{1,0:T(8,128)(2,1)}, u32[]{:S(2)}) copy-start(bf16[1792,128]{1,0:T(8,128)(2,1)} %copy-done.6) | copy-start | bytes 1376260 | tf_op jit(solution)/shard_map/while
  171.5 3.3 %copy-start.9 = (bf16[6,2,256,128]{3,2,1,0:T(8,128)(2,1)S(1)}, bf16[6,2,256,128]{3,2,1,0:T(8,128)(2,1)}, u32[]{:S(2)}) copy-start(bf16[6,2,256,128]{3,2,1,0:T(8,128)(2,1)} %copy-done.8) | copy-start | bytes 2359300 | tf_op jit(solution)/shard_map/while
  174.8 3.6 %copy-start.8 = (bf16[6,2,256,128]{3,2,1,0:T(8,128)(2,1)}, bf16[6,2,256,128]{3,2,1,0:T(8,128)(2,1)S(1)}, u32[]{:S(2)}) copy-start(bf16[6,2,256,128]{3,2,1,0:T(8,128)(2,1)S(1)} %get-tuple-element.236) | copy-start | bytes 2359300 | tf_op jit(solution)/shard_map/while
  182.8 3.3 %copy-start.5 = (pred[256,1792]{1,0:T(8,128)(4,1)S(1)}, pred[256,1792]{1,0:T(8,128)(4,1)}, u32[]{:S(2)}) copy-start(pred[256,1792]{1,0:T(8,128)(4,1)} %copy-done.4) | copy-start | bytes 1376260 | tf_op jit(solution)/shard_map/while
  182.8 3.3 %copy-start.7 = (bf16[1792,128]{1,0:T(8,128)(2,1)S(1)}, bf16[1792,128]{1,0:T(8,128)(2,1)}, u32[]{:S(2)}) copy-start(bf16[1792,128]{1,0:T(8,128)(2,1)} %copy-done.6) | copy-start | bytes 1376260 | tf_op jit(solution)/shard_map/while
  182.9 3.3 %copy-start.9 = (bf16[6,2,256,128]{3,2,1,0:T(8,128)(2,1)S(1)}, bf16[6,2,256,128]{3,2,1,0:T(8,128)(2,1)}, u32[]{:S(2)}) copy-start(bf16[6,2,256,128]{3,2,1,0:T(8,128)(2,1)} %copy-done.8) | copy-start | bytes 2359300 | tf_op jit(solution)/shard_map/while
  186.2 3.6 %copy-start.8 = (bf16[6,2,256,128]{3,2,1,0:T(8,128)(2,1)}, bf16[6,2,256,128]{3,2,1,0:T(8,128)(2,1)S(1)}, u32[]{:S(2)}) copy-start(bf16[6,2,256,128]{3,2,1,0:T(8,128)(2,1)S(1)} %get-tuple-element.236) | copy-start | bytes 2359300 | tf_op jit(solution)/shard_map/while
  194.2 3.3 %copy-start.5 = (pred[256,1792]{1,0:T(8,128)(4,1)S(1)}, pred[256,1792]{1,0:T(8,128)(4,1)}, u32[]{:S(2)}) copy-start(pred[256,1792]{1,0:T(8,128)(4,1)} %copy-done.4) | copy-start | bytes 1376260 | tf_op jit(solution)/shard_map/while
  194.2 3.3 %copy-start.7 = (bf16[1792,128]{1,0:T(8,128)(2,1)S(1)}, bf16[1792,128]{1,0:T(8,128)(2,1)}, u32[]{:S(2)}) copy-start(bf16[1792,128]{1,0:T(8,128)(2,1)} %copy-done.6) | copy-start | bytes 1376260 | tf_op jit(solution)/shard_map/while
  194.2 3.3 %copy-start.9 = (bf16[6,2,256,128]{3,2,1,0:T(8,128)(2,1)S(1)}, bf16[6,2,256,128]{3,2,1,0:T(8,128)(2,1)}, u32[]{:S(2)}) copy-start(bf16[6,2,256,128]{3,2,1,0:T(8,128)(2,1)} %copy-done.8) | copy-start | bytes 2359300 | tf_op jit(solution)/shard_map/while
  197.6 3.6 %copy-start.8 = (bf16[6,2,256,128]{3,2,1,0:T(8,128)(2,1)}, bf16[6,2,256,128]{3,2,1,0:T(8,128)(2,1)S(1)}, u32[]{:S(2)}) copy-start(bf16[6,2,256,128]{3,2,1,0:T(8,128)(2,1)S(1)} %get-tuple-element.236) | copy-start | bytes 2359300 | tf_op jit(solution)/shard_map/while
  205.6 3.3 %copy-start.5 = (pred[256,1792]{1,0:T(8,128)(4,1)S(1)}, pred[256,1792]{1,0:T(8,128)(4,1)}, u32[]{:S(2)}) copy-start(pred[256,1792]{1,0:T(8,128)(4,1)} %copy-done.4) | copy-start | bytes 1376260 | tf_op jit(solution)/shard_map/while
  205.6 3.3 %copy-start.7 = (bf16[1792,128]{1,0:T(8,128)(2,1)S(1)}, bf16[1792,128]{1,0:T(8,128)(2,1)}, u32[]{:S(2)}) copy-start(bf16[1792,128]{1,0:T(8,128)(2,1)} %copy-done.6) | copy-start | bytes 1376260 | tf_op jit(solution)/shard_map/while
  205.6 3.3 %copy-start.9 = (bf16[6,2,256,128]{3,2,1,0:T(8,128)(2,1)S(1)}, bf16[6,2,256,128]{3,2,1,0:T(8,128)(2,1)}, u32[]{:S(2)}) copy-start(bf16[6,2,256,128]{3,2,1,0:T(8,128)(2,1)} %copy-done.8) | copy-start | bytes 2359300 | tf_op jit(solution)/shard_map/while
  210.2 7.2 %copy-start.10 = (f32[1792,256]{1,0:T(8,128)}, f32[1792,256]{1,0:T(8,128)S(1)}, u32[]{:S(2)}) copy-start(f32[1792,256]{1,0:T(8,128)S(1)} %constant_dynamic-update-slice_fusion.29) | copy-start | bytes 5505028
  212.0 51.2 %collective-permute-start.11 = (f32[256,256]{1,0:T(8,128)}, f32[256,256]{1,0:T(8,128)S(1)}, u32[]{:S(2)}, u32[]{:S(2)}) collective-permute-start(f32[256,256]{1,0:T(8,128)} %get-tuple-element.124), channel_id=1, source_target_pairs={{4,0},{8,4},{12,8},{16,12},{20,16},{24,20},{28,24},{5,1},{9,5},{13... | collective-permute-start | bytes 786440 | tf_op jit(solution)/shard_map/ppermute | solution.py:14
  213.3 49.9 %collective-permute-start.12 = (f32[256,256]{1,0:T(8,128)}, f32[256,256]{1,0:T(8,128)S(1)}, u32[]{:S(2)}, u32[]{:S(2)}) collective-permute-start(f32[256,256]{1,0:T(8,128)} %get-tuple-element.127), channel_id=1, source_target_pairs={{8,0},{12,4},{16,8},{20,12},{24,16},{28,20},{9,1},{13,5},{17,9},{2... | collective-permute-start | bytes 786440 | tf_op jit(solution)/shard_map/ppermute | solution.py:14
  214.6 48.6 %collective-permute-start.13 = (f32[256,256]{1,0:T(8,128)}, f32[256,256]{1,0:T(8,128)}, u32[]{:S(2)}, u32[]{:S(2)}) collective-permute-start(f32[256,256]{1,0:T(8,128)} %get-tuple-element.126), channel_id=1, source_target_pairs={{12,0},{16,4},{20,8},{24,12},{28,16},{13,1},{17,5},{21,9},{25,13},... | collective-permute-start | bytes 786440 | tf_op jit(solution)/shard_map/ppermute | solution.py:14
  215.9 47.3 %collective-permute-start.14 = (f32[256,256]{1,0:T(8,128)}, f32[256,256]{1,0:T(8,128)}, u32[]{:S(2)}, u32[]{:S(2)}) collective-permute-start(f32[256,256]{1,0:T(8,128)} %get-tuple-element.125), channel_id=1, source_target_pairs={{16,0},{20,4},{24,8},{28,12},{17,1},{21,5},{25,9},{29,13},{18,2},{... | collective-permute-start | bytes 786440 | tf_op jit(solution)/shard_map/ppermute | solution.py:14
  221.1 53.1 %all-to-all-start.4 = ((f32[4,64,1536]{2,1,0:T(8,128)}), f32[4,64,1536]{2,1,0:T(8,128)S(1)}, u32[]{:S(2)}, u32[]{:S(2)}) async-start(f32[4,64,1536]{2,1,0:T(8,128)} %all_to_all.108), calls=%async_computation.4 | async-start | bytes 3145728 | tf_op jit(solution)/shard_map/all_to_all | solution.py:184
  274.2 7.9 %all-to-all-start.6 = ((f32[4,64,128]{2,1,0:T(8,128)}), f32[4,64,128]{2,1,0:T(8,128)S(1)}, u32[]{:S(2)}, u32[]{:S(2)}) async-start(f32[4,64,128]{2,1,0:T(8,128)} %bitcast.29), calls=%async_computation.6 | async-start | bytes 262144 | tf_op jit(solution)/shard_map/all_to_all | solution.py:186
  282.1 7.9 %all-to-all-start.5 = ((f32[4,64,128]{2,1,0:T(8,128)}), f32[4,64,128]{2,1,0:T(8,128)S(1)}, u32[]{:S(2)}, u32[]{:S(2)}) async-start(f32[4,64,128]{2,1,0:T(8,128)} %bitcast.27), calls=%async_computation.5 | async-start | bytes 262144 | tf_op jit(solution)/shard_map/all_to_all | solution.py:185
  (27 other events, 56.4 us)
Sparse Core Ops, SparseCore 0:
  211.1 58.9 all-gather.1
